TPU v7x, 32 devices: a whole 2x2x4 slice. The times are simulated.
32 devices in a mesh: hyd: 4 (over y, x), src: 8 (over z, core).
Axes of the slice: x: 2, y: 2, z: 4, core: 2. Of those that a mesh axis runs over, the one named last changes fastest.
Arguments:
- record: float32 [2, 4096, 128], P(None, 'hyd'), may hold values from -6 to 6
- tile_data: bfloat16 [4, 8, 24, 2, 128, 128], P('hyd', 'src'), may hold values from -0.125 to 0.125
- tile_rows: int32 [4, 8, 24], P('hyd', 'src'), may hold values from 0 to 7, as said below
- tile_cols: int32 [4, 8, 24], P('hyd', 'src'), may hold values from 0 to 7, as said below
- tile_counts: int32 [4, 8], P('hyd', 'src'), may hold values from 3 to 24, as said below
Outputs:
- solution: float32 [2, 8192, 128], P(None, 'src')
- residual: float32 [2, 4096, 128], P(None, 'hyd')
Inputs may be any that keep to these rules, and one draw needn't show every extreme that they name: `tile_rows`: together with tile_cols, the 24 slots of one device name different tile pairs. `tile_cols`: column tiles below 4 belong to the upper layer. `tile_counts`: slots at and beyond a device's count hold no tiles of A.
All inputs are finite; a program needn't handle non-finite values.
Results may differ from a plain program's by a relative error of at most 0.014.
Values may be sent and summed in bfloat16 or wider, within the bound.
No kernel may reach another device: no remote copies, remote signals or barrier semaphores. Data moves between devices by JAX's collectives and lax.ppermute only.
A program may use at most 64 MiB of HBM per device.

v0:
```python
import jax
import jax.numpy as jnp
from jax import lax
from jax.sharding import PartitionSpec as P

SRC_DEV = 512
ITERS = 3
EPSILON = 1e-06


def place_tiles(total, products, target, usable):
    for slot in range(products.shape[1]):
        current = lax.dynamic_slice_in_dim(total, target[slot], 1, 1)
        added = current + products[:, slot][:, None] * usable[slot]
        total = lax.dynamic_update_slice_in_dim(total, added, target[slot], 1)
    return total


def tile_forward(tile_group_all, rows_list, cols_list, first_slot, end_slot, vector_b, row_tiles):
    group_slots = 8
    tile_size = tile_group_all.shape[-1]
    shot_count = vector_b.shape[2]
    col_tiles = vector_b.shape[1] // tile_size
    blocks = vector_b.reshape(2, col_tiles, tile_size, shot_count)

    def one_turn(group, total):
        start = group * group_slots
        tile_group = lax.dynamic_slice_in_dim(tile_group_all, start, group_slots, 0)
        col_pick = lax.dynamic_slice_in_dim(cols_list, start, group_slots, 0)
        row_pick = lax.dynamic_slice_in_dim(rows_list, start, group_slots, 0)
        slot_ids = start + jnp.arange(group_slots)
        usable = ((slot_ids >= first_slot) & (slot_ids < end_slot)).astype(jnp.float32)
        chosen = jnp.take(blocks, col_pick, axis=1)
        real_part = jnp.einsum(
            "gij,gjn->gin", tile_group[:, 0], chosen[0], preferred_element_type=jnp.float32
        ) - jnp.einsum(
            "gij,gjn->gin", tile_group[:, 1], chosen[1], preferred_element_type=jnp.float32
        )
        imag_part = jnp.einsum(
            "gij,gjn->gin", tile_group[:, 0], chosen[1], preferred_element_type=jnp.float32
        ) + jnp.einsum(
            "gij,gjn->gin", tile_group[:, 1], chosen[0], preferred_element_type=jnp.float32
        )
        return place_tiles(total, jnp.stack([real_part, imag_part]), row_pick, usable)

    empty = jnp.zeros((2, row_tiles, tile_size, shot_count), jnp.float32)
    result = lax.fori_loop(
        first_slot // group_slots, (end_slot + group_slots - 1) // group_slots, one_turn, empty
    )
    return result.reshape(2, row_tiles * tile_size, shot_count)


def tile_adjoint(tile_group_all, rows_list, cols_list, first_slot, end_slot, residual_b, col_tiles):
    group_slots = 8
    tile_size = tile_group_all.shape[-1]
    shot_count = residual_b.shape[2]
    row_tiles = residual_b.shape[1] // tile_size
    blocks = residual_b.reshape(2, row_tiles, tile_size, shot_count)

    def one_turn(group, total):
        start = group * group_slots
        tile_group = lax.dynamic_slice_in_dim(tile_group_all, start, group_slots, 0)
        col_pick = lax.dynamic_slice_in_dim(cols_list, start, group_slots, 0)
        row_pick = lax.dynamic_slice_in_dim(rows_list, start, group_slots, 0)
        slot_ids = start + jnp.arange(group_slots)
        usable = ((slot_ids >= first_slot) & (slot_ids < end_slot)).astype(jnp.float32)
        chosen = jnp.take(blocks, row_pick, axis=1)
        real_part = jnp.einsum(
            "gji,gjn->gin", tile_group[:, 0], chosen[0], preferred_element_type=jnp.float32
        ) + jnp.einsum(
            "gji,gjn->gin", tile_group[:, 1], chosen[1], preferred_element_type=jnp.float32
        )
        imag_part = jnp.einsum(
            "gji,gjn->gin", tile_group[:, 0], chosen[1], preferred_element_type=jnp.float32
        ) - jnp.einsum(
            "gji,gjn->gin", tile_group[:, 1], chosen[0], preferred_element_type=jnp.float32
        )
        return place_tiles(total, jnp.stack([real_part, imag_part]), col_pick, usable)

    empty = jnp.zeros((2, col_tiles, tile_size, shot_count), jnp.float32)
    result = lax.fori_loop(
        first_slot // group_slots, (end_slot + group_slots - 1) // group_slots, one_turn, empty
    )
    return result.reshape(2, col_tiles * tile_size, shot_count)


def body(record, tile_data, tile_rows, tile_cols, tile_counts):
    own_tiles = tile_data[0, 0]
    own_rows = tile_rows[0, 0]
    own_cols = tile_cols[0, 0]
    own_count = tile_counts[0, 0]
    tile_size = own_tiles.shape[-1]
    row_tiles = record.shape[1] // tile_size
    col_tiles = 2 * SRC_DEV // tile_size

    def gradient_of(residual_b):
        partial_value = tile_adjoint(
            own_tiles, own_rows, own_cols, 0, own_count, residual_b, col_tiles
        )
        gradient = lax.psum(partial_value, "hyd")
        squares = lax.psum(jnp.sum(gradient * gradient, axis=(0, 1)), "src")
        return (gradient, squares)

    residual = record
    gradient, gamma_now = gradient_of(record.astype(jnp.bfloat16))
    direction = gradient
    solution = jnp.zeros_like(gradient)
    for step_index in range(ITERS):
        direction_b = direction.astype(jnp.bfloat16)
        forward_partial_value = tile_forward(
            own_tiles, own_rows, own_cols, 0, own_count, direction_b, row_tiles
        )
        image = lax.psum(forward_partial_value, "src")
        image_sq = lax.psum(jnp.sum(image * image, axis=(0, 1)), "hyd")
        image, image_sq = (image, image_sq)
        alpha_step = gamma_now / (image_sq + EPSILON)
        solution = solution + alpha_step * direction
        residual = residual - alpha_step * image
        if step_index + 1 < ITERS:
            residual_b = residual.astype(jnp.bfloat16)
            gradient, gamma_next = gradient_of(residual_b)
            direction = gradient + gamma_next / (gamma_now + EPSILON) * direction
            gamma_now = gamma_next
    return (solution, residual)


def solution(mesh):
    in_specs = (
        P(None, "hyd", None),
        P("hyd", "src", None, None, None, None),
        P("hyd", "src", None),
        P("hyd", "src", None),
        P("hyd", "src"),
    )
    out_specs = (P(None, "src", None), P(None, "hyd", None))
    return jax.shard_map(body, mesh=mesh, in_specs=in_specs, out_specs=out_specs, check_vma=False)
```

profile of v0, /device:TPU:0, one launch (start us, length us, event | category | flops | bytes accessed | tf_op | source)
XLA Modules:
  0.0 1104.4 jit_solution(888676539581461893)
XLA Ops:
  7.9 2.7 copy.18
  11.3 28.1 %while.60 = (s32[]{:T(128)}, f32[2,8,128,128]{3,2,1,0:T(8,128)S(1)}, s32[]{:T(128)}, s32[24]{0:T(128)S(1)}, bf16[24,2,128,128]{2,3,0,1:T(8,128)(2,1)}, /*index=5...) while((s32[]{:T(128)}, ...), condition=%wide.region_1.3_spmd, body=%wide.region_0.2_spmd.sunk | while | flops 135529568 | bytes 17830816 | solution.py:81
  41.9 108.4 %all-reduce.7.cloned.1.call-done = f32[2,1024,128]{2,1,0:T(8,128)} async-done(((f32[2,1024,128]{2,1,0:T(8,128)}), f32[2,1024,128]{2,1,0:T(8,128)}) %all-reduce.7.cloned.1.call-update) | async-done | bytes 1048592 | tf_op jit(solution)/shard_map/psum | solution.py:100
  150.3 2.5 multiply_reduce_fusion.5
  153.9 38.0 %while.61 = (s32[]{:T(128)}, f32[2,8,128,128]{3,2,1,0:T(8,128)}, s32[]{:T(128)}, s32[24]{0:T(128)S(1)}, bf16[24,2,128,128]{3,2,0,1:T(8,128)(2,1)S(1)}, /*index=5...) while((s32[]{:T(128)}, f32[2,8,128,128]{3,2,1,0:T(8,128)}, ...), condition=%wide.region_6.8_spmd, body=%wide.region_5.7_spmd.sunk | while | flops 135529568 | bytes 17834880 | solution.py:47
  160.6 2.3 fusion.368
  164.8 2.2 fusion.369
  169.1 2.1 fusion.370
  173.1 2.1 fusion.371
  177.4 2.2 fusion.372
  181.6 2.2 fusion.373
  185.8 2.3 fusion.374
  189.8 2.2 fusion.375
  192.0 92.6 %psum.85 = f32[128]{0:T(128)S(1)} all-reduce(f32[128]{0:T(128)S(1)} %get-tuple-element.527), channel_id=1, replica_groups=mesh['hyd'=4,'src'=8] {'src'}, use_global_device_ids=true, to_apply=%region_4.6 | all-reduce | flops 128 | bytes 1024 | tf_op jit(solution)/shard_map/psum | solution.py:101
  284.6 42.1 %all-reduce.9.cloned.1.call-done = f32[2,1024,128]{2,1,0:T(8,128)} async-done(((f32[2,1024,128]{2,1,0:T(8,128)}), f32[2,1024,128]{2,1,0:T(8,128)}) %all-reduce.9.cloned.1.call-update) | async-done | bytes 1048592 | tf_op jit(solution)/shard_map/psum | solution.py:113
  328.2 9.8 psum.87
  338.0 2.1 fusion.241
  341.2 41.8 %while.62 = (s32[]{:T(128)}, f32[2,8,128,128]{3,2,1,0:T(8,128)}, s32[]{:T(128)}, s32[24]{0:T(128)S(1)}, bf16[24,2,128,128]{2,3,0,1:T(8,128)(2,1)}, /*index=5*/s3...) while((s32[]{:T(128)}, f32[2,8,128,128]{3,2,1,0:T(8,128)}, ...), condition=%wide.region_11.13_spmd, body=%wide.region_10.12_spmd.sunk | while | flops 135529568 | bytes 17834880 | solution.py:81
  351.6 2.3 fusion.383
  355.9 2.2 fusion.384
  360.2 2.1 fusion.385
  364.2 2.1 fusion.386
  368.4 2.2 fusion.387
  372.7 2.2 fusion.388
  376.9 2.3 fusion.389
  380.8 2.2 fusion.390
  383.1 132.6 %all-reduce.11.cloned.1.call-done = f32[2,1024,128]{2,1,0:T(8,128)} async-done(((f32[2,1024,128]{2,1,0:T(8,128)}), f32[2,1024,128]{2,1,0:T(8,128)}) %all-reduce.11.cloned.1.call-update) | async-done | bytes 1048592 | tf_op jit(solution)/shard_map/psum | solution.py:100
  517.2 16.2 %psum.89 = f32[128]{0:T(128)S(1)} all-reduce(f32[128]{0:T(128)S(1)} %multiply_reduce_fusion.3), channel_id=1, replica_groups=mesh['hyd'=4,'src'=8] {'src'}, use_global_device_ids=true, to_apply=%region_14.16 | all-reduce | flops 128 | bytes 1024 | tf_op jit(solution)/shard_map/psum | solution.py:101
  533.4 2.1 fusion.242
  536.6 38.0 %while.63 = (s32[]{:T(128)}, f32[2,8,128,128]{3,2,1,0:T(8,128)}, s32[]{:T(128)}, s32[24]{0:T(128)S(1)}, bf16[24,2,128,128]{3,2,0,1:T(8,128)(2,1)S(1)}, /*index=5...) while((s32[]{:T(128)}, f32[2,8,128,128]{3,2,1,0:T(8,128)}, ...), condition=%wide.region_16.18_spmd, body=%wide.region_15.17_spmd.sunk | while | flops 135529568 | bytes 17834880 | solution.py:47
  543.6 2.2 fusion.398
  547.8 2.2 fusion.399
  552.0 2.2 fusion.400
  556.1 2.3 fusion.401
  564.2 2.2 fusion.403
  568.2 2.1 fusion.404
  572.3 2.3 fusion.405
  574.7 131.5 %all-reduce.13.cloned.1.call-done = f32[2,1024,128]{2,1,0:T(8,128)} async-done(((f32[2,1024,128]{2,1,0:T(8,128)}), f32[2,1024,128]{2,1,0:T(8,128)}) %all-reduce.13.cloned.1.call-update) | async-done | bytes 1048592 | tf_op jit(solution)/shard_map/psum | solution.py:113
  707.7 9.8 psum.91
  717.5 2.9 fusion.243
  721.4 41.1 %while.64 = (s32[]{:T(128)}, f32[2,8,128,128]{3,2,1,0:T(8,128)}, s32[]{:T(128)}, s32[24]{0:T(128)S(1)}, bf16[24,2,128,128]{2,3,0,1:T(8,128)(2,1)}, /*index=5*/s3...) while((s32[]{:T(128)}, f32[2,8,128,128]{3,2,1,0:T(8,128)}, ...), condition=%wide.region_21.23_spmd, body=%wide.region_20.22_spmd.sunk | while | flops 135529568 | bytes 17834880 | solution.py:81
  732.0 2.2 fusion.413
  736.0 2.3 fusion.414
  740.0 2.2 fusion.415
  743.9 2.1 fusion.416
  748.1 2.2 fusion.417
  752.1 2.2 fusion.418
  756.1 2.3 fusion.419
  760.3 2.2 fusion.420
  762.6 131.3 %all-reduce.15.cloned.1.call-done = f32[2,1024,128]{2,1,0:T(8,128)} async-done(((f32[2,1024,128]{2,1,0:T(8,128)}), f32[2,1024,128]{2,1,0:T(8,128)}) %all-reduce.15.cloned.1.call-update) | async-done | bytes 1048592 | tf_op jit(solution)/shard_map/psum | solution.py:100
  895.4 16.2 %psum.93 = f32[128]{0:T(128)S(1)} all-reduce(f32[128]{0:T(128)S(1)} %multiply_reduce_fusion.1), channel_id=1, replica_groups=mesh['hyd'=4,'src'=8] {'src'}, use_global_device_ids=true, to_apply=%region_24.26 | all-reduce | flops 128 | bytes 1024 | tf_op jit(solution)/shard_map/psum | solution.py:101
  911.6 2.5 fusion.240
  915.2 37.3 %while.65 = (s32[]{:T(128)}, f32[2,8,128,128]{3,2,1,0:T(8,128)}, s32[]{:T(128)}, s32[24]{0:T(128)S(1)}, bf16[24,2,128,128]{3,2,0,1:T(8,128)(2,1)S(1)}, /*index=5...) while((s32[]{:T(128)}, f32[2,8,128,128]{3,2,1,0:T(8,128)}, ...), condition=%wide.region_26.28_spmd, body=%wide.region_25.27_spmd.sunk | while | flops 135529568 | bytes 17834880 | solution.py:47
  921.9 2.2 fusion.428
  926.0 2.3 fusion.429
  930.0 2.2 fusion.430
  933.8 2.1 fusion.431
  938.0 2.2 fusion.432
  942.1 2.2 fusion.433
  946.1 2.3 fusion.434
  950.3 2.2 fusion.435
  952.5 130.2 %all-reduce.17.cloned.1.call-done = f32[2,1024,128]{2,1,0:T(8,128)} async-done(((f32[2,1024,128]{2,1,0:T(8,128)}), f32[2,1024,128]{2,1,0:T(8,128)}) %all-reduce.17.cloned.1.call-update) | async-done | bytes 1048592 | tf_op jit(solution)/shard_map/psum | solution.py:113
  1084.2 9.8 psum.95
  1094.0 3.6 multiply_subtract_fusion
  (125 shorter events, 63.3 us)
Async XLA Ops:
  7.2 143.2 %all-reduce.7.cloned.1.call-start = ((), (), s32[]{:S(2)}) async-start(), calls=%async_computation | async-start | bytes 2097152 | tf_op jit(solution)/shard_map/psum | solution.py:100
  7.9 2.7 copy-start.5
  10.6 0.7 copy-start.8
  10.6 0.7 copy-start.9
  39.3 1.0 copy-start
  40.3 286.4 %all-reduce.9.cloned.1.call-start = ((), (), s32[]{:S(2)}) async-start(), calls=%async_computation.1 | async-start | bytes 2097152 | tf_op jit(solution)/shard_map/psum | solution.py:113
  191.9 146.1 %copy-start.6 = (f32[2,1024,128]{2,1,0:T(8,128)S(1)}, f32[2,1024,128]{2,1,0:T(8,128)}, u32[]{:S(2)}) copy-start(f32[2,1024,128]{2,1,0:T(8,128)} %param.19) | copy-start | bytes 3145732
  192.0 323.8 %all-reduce.11.cloned.1.call-start = ((), (), s32[]{:S(2)}) async-start(), calls=%async_computation.2 | async-start | bytes 2097152 | tf_op jit(solution)/shard_map/psum | solution.py:100
  383.0 150.4 %copy-start.1 = (f32[2,1024,128]{2,1,0:T(8,128)S(1)}, f32[2,1024,128]{2,1,0:T(8,128)}, u32[]{:S(2)}) copy-start(f32[2,1024,128]{2,1,0:T(8,128)} %all-reduce.7.cloned.1.call-done) | copy-start | bytes 3145732
  383.0 323.1 %all-reduce.13.cloned.1.call-start = ((), (), s32[]{:S(2)}) async-start(), calls=%async_computation.3 | async-start | bytes 2097152 | tf_op jit(solution)/shard_map/psum | solution.py:113
  574.6 142.8 %copy-start.7 = (f32[2,1024,128]{2,1,0:T(8,128)S(1)}, f32[2,1024,128]{2,1,0:T(8,128)}, u32[]{:S(2)}) copy-start(f32[2,1024,128]{2,1,0:T(8,128)} %param.19) | copy-start | bytes 3145732
  574.6 319.2 %all-reduce.15.cloned.1.call-start = ((), (), s32[]{:S(2)}) async-start(), calls=%async_computation.4 | async-start | bytes 2097152 | tf_op jit(solution)/shard_map/psum | solution.py:100
  762.5 149.0 %copy-start.2 = (f32[2,1024,128]{2,1,0:T(8,128)S(1)}, f32[2,1024,128]{2,1,0:T(8,128)}, u32[]{:S(2)}) copy-start(f32[2,1024,128]{2,1,0:T(8,128)} %all-reduce.7.cloned.1.call-done) | copy-start | bytes 3145732
  762.6 320.1 %all-reduce.17.cloned.1.call-start = ((), (), s32[]{:S(2)}) async-start(), calls=%async_computation.5 | async-start | bytes 2097152 | tf_op jit(solution)/shard_map/psum | solution.py:113
  952.5 141.5 %copy-start.3 = (f32[2,1024,128]{2,1,0:T(8,128)S(1)}, f32[2,1024,128]{2,1,0:T(8,128)}, u32[]{:S(2)}) copy-start(f32[2,1024,128]{2,1,0:T(8,128)} %all-reduce.7.cloned.1.call-done) | copy-start | bytes 3145732
  952.5 141.5 %copy-start.4 = (f32[2,1024,128]{2,1,0:T(8,128)S(1)}, f32[2,1024,128]{2,1,0:T(8,128)}, u32[]{:S(2)}) copy-start(f32[2,1024,128]{2,1,0:T(8,128)} %all-reduce.11.cloned.1.call-done) | copy-start | bytes 3145732
Sparse Core Ops, SparseCore 0:
  40.4 109.8 all-reduce.6
  192.1 134.5 all-reduce.8
  383.1 132.5 all-reduce.10
  574.8 131.3 all-reduce.12
  762.7 131.1 all-reduce.14
  952.6 130.0 all-reduce.16
where the time goes:
time: 1110 us; the launch traced here: 1100 us
  waiting for transfers between devices  676 us (61%)
  blocking collectives  154 us (14%)
  other arithmetic  122 us (11%)
  loops' own time  91.6 us (8%)
  local copies, waits for them, and re-layouts  29 us (3%)
  matrix products  16.7 us (2%)
  between operations  14.9 us (1%)
    psum x3, waiting for transfers between devices, gradient_of(): gradient = lax.psum(partial_value, 'hyd')  372 us
    psum x3, waiting for transfers between devices, body(): image = lax.psum(forward_partial_value, 'src')  304 us
    psum x3, blocking collectives, gradient_of(): squares = lax.psum(jnp.sum(gradient * gradient, axis=(0, 1)), 'src')  125 us
    dynamic_update_slice x48, other arithmetic, place_tiles(): total = lax.dynamic_update_slice_in_dim(total, added, target[slot], 1)  93.1 us
    another operation x3, loops' own time, tile_forward(): lax.fori_loop(first_slot // group_slots, (end_slot + group_slots - 1) //...  45.9 us
    another operation x3, loops' own time, tile_adjoint(): lax.fori_loop(first_slot // group_slots, (end_slot + group_slots - 1) //...  45.7 us
    psum x3, blocking collectives, body(): image_sq = lax.psum(jnp.sum(image * image, axis=(0, 1)), 'hyd')  29.3 us
  transfers between devices with their start and end apart: 6, of which 6 were waited for; matrix products, arithmetic and copies ran while one was open for 0% of the time, Pallas kernels for 0%

commit v1 on v0

--- a/solution.py
+++ b/solution.py
@@ -110,7 +110,7 @@
         forward_partial_value = tile_forward(
             own_tiles, own_rows, own_cols, 0, own_count, direction_b, row_tiles
         )
-        image = lax.psum(forward_partial_value, "src")
+        image = jnp.sum(lax.all_gather(forward_partial_value, "src"), axis=0)
         image_sq = lax.psum(jnp.sum(image * image, axis=(0, 1)), "hyd")
         image, image_sq = (image, image_sq)
         alpha_step = gamma_now / (image_sq + EPSILON)

time: 1110 us -> 1190 us (1.072)
  waiting for transfers between devices: 676 us -> 739 us
  other arithmetic: 122 us -> 134 us
    all_gather x0 -> x3, waiting for transfers between devices: none -> 371 us  [body(): image = jnp.sum(lax.all_gather(forward_partial_value, 'src'), axis=0)]
    psum x3 -> x0, waiting for transfers between devices: 304 us -> none  [body(): image = lax.psum(forward_partial_value, 'src')]
    reduce_sum x0 -> x3, other arithmetic: none -> 13.7 us  [body(): image = jnp.sum(lax.all_gather(forward_partial_value, 'src'), axis=0)]
where the time goes in v1:
time: 1190 us; the launch traced here: 1180 us
  waiting for transfers between devices  739 us (62%)
  blocking collectives  154 us (13%)
  other arithmetic  134 us (11%)
  loops' own time  90.2 us (8%)
  local copies, waits for them, and re-layouts  28.9 us (2%)
  matrix products  16.7 us (1%)
  between operations  14.9 us (1%)
    all_gather x3, waiting for transfers between devices, body(): image = jnp.sum(lax.all_gather(forward_partial_value, 'src'), axis=0)  371 us
    psum x3, waiting for transfers between devices, gradient_of(): gradient = lax.psum(partial_value, 'hyd')  367 us
    psum x3, blocking collectives, gradient_of(): squares = lax.psum(jnp.sum(gradient * gradient, axis=(0, 1)), 'src')  124 us
    dynamic_update_slice x48, other arithmetic, place_tiles(): total = lax.dynamic_update_slice_in_dim(total, added, target[slot], 1)  93.2 us
    another operation x3, loops' own time, tile_forward(): lax.fori_loop(first_slot // group_slots, (end_slot + group_slots - 1) //...  45.1 us
    another operation x3, loops' own time, tile_adjoint(): lax.fori_loop(first_slot // group_slots, (end_slot + group_slots - 1) //...  45 us
    psum x3, blocking collectives, body(): image_sq = lax.psum(jnp.sum(image * image, axis=(0, 1)), 'hyd')  29.5 us
  transfers between devices with their start and end apart: 6, of which 6 were waited for; matrix products, arithmetic and copies ran while one was open for 0% of the time, Pallas kernels for 0%

profile of v1, /device:TPU:0, one launch (start us, length us, event | category | flops | bytes accessed | tf_op | source)
XLA Modules:
  0.0 1177.6 jit_solution(13305303398001013003)
XLA Ops:
  7.9 2.7 copy.28
  11.3 27.7 %while.60 = (s32[]{:T(128)}, f32[2,8,128,128]{3,2,1,0:T(8,128)S(1)}, s32[]{:T(128)}, s32[24]{0:T(128)S(1)}, bf16[24,2,128,128]{2,3,0,1:T(8,128)(2,1)}, /*index=5...) while((s32[]{:T(128)}, ...), condition=%wide.region_1.3_spmd, body=%wide.region_0.2_spmd.sunk | while | flops 135529568 | bytes 17830816 | solution.py:81
  41.7 107.7 %all-reduce.4.cloned.1.call-done = f32[2,1024,128]{2,1,0:T(8,128)} async-done(((f32[2,1024,128]{2,1,0:T(8,128)}), f32[2,1024,128]{2,1,0:T(8,128)}) %all-reduce.4.cloned.1.call-update) | async-done | bytes 1048592 | tf_op jit(solution)/shard_map/psum | solution.py:100
  149.4 2.6 multiply_reduce_fusion.5
  153.1 37.5 %while.61 = (s32[]{:T(128)}, f32[2,8,128,128]{3,2,1,0:T(8,128)}, s32[]{:T(128)}, s32[24]{0:T(128)S(1)}, bf16[24,2,128,128]{3,2,0,1:T(8,128)(2,1)S(1)}, /*index=5...) while((s32[]{:T(128)}, f32[2,8,128,128]{3,2,1,0:T(8,128)}, ...), condition=%wide.region_6.8_spmd, body=%wide.region_5.7_spmd.sunk | while | flops 135529568 | bytes 17834880 | solution.py:47
  160.0 2.2 fusion.368
  164.0 2.3 fusion.369
  168.1 2.2 fusion.370
  172.0 2.2 fusion.371
  176.1 2.1 fusion.372
  180.1 2.2 fusion.373
  184.2 2.2 fusion.374
  188.4 2.3 fusion.375
  190.7 91.9 %psum.64 = f32[128]{0:T(128)S(1)} all-reduce(f32[128]{0:T(128)S(1)} %get-tuple-element.551), channel_id=1, replica_groups=mesh['hyd'=4,'src'=8] {'src'}, use_global_device_ids=true, to_apply=%region_4.6 | all-reduce | flops 128 | bytes 1024 | tf_op jit(solution)/shard_map/psum | solution.py:101
  282.6 64.7 %all-gather.4.cloned.1.call-done = f32[8,2,1024,128]{3,2,1,0:T(8,128)} async-done(((f32[1,2,1024,128]{3,2,1,0:T(8,128)}), f32[8,2,1024,128]{3,2,1,0:T(8,128)}) %all-gather.4.cloned.1.call-update) | async-done | bytes 8388624 | tf_op jit(solution)/shard_map/all_gather | solution.py:113
  347.3 3.9 reduce_sum.82
  351.5 9.8 psum.65
  364.5 41.4 %while.62 = (s32[]{:T(128)}, f32[2,8,128,128]{3,2,1,0:T(8,128)}, s32[]{:T(128)}, s32[24]{0:T(128)S(1)}, bf16[24,2,128,128]{2,3,0,1:T(8,128)(2,1)}, /*index=5*/s3...) while((s32[]{:T(128)}, f32[2,8,128,128]{3,2,1,0:T(8,128)}, ...), condition=%wide.region_11.13_spmd, body=%wide.region_10.12_spmd.sunk | while | flops 135529568 | bytes 17834880 | solution.py:81
  375.2 2.2 fusion.383
  379.2 2.3 fusion.384
  383.4 2.2 fusion.385
  387.3 2.2 fusion.386
  391.4 2.1 fusion.387
  395.4 2.2 fusion.388
  399.4 2.2 fusion.389
  403.6 2.3 fusion.390
  405.9 130.1 %all-reduce.6.cloned.1.call-done = f32[2,1024,128]{2,1,0:T(8,128)} async-done(((f32[2,1024,128]{2,1,0:T(8,128)}), f32[2,1024,128]{2,1,0:T(8,128)}) %all-reduce.6.cloned.1.call-update) | async-done | bytes 1048592 | tf_op jit(solution)/shard_map/psum | solution.py:100
  537.5 16.2 %psum.67 = f32[128]{0:T(128)S(1)} all-reduce(f32[128]{0:T(128)S(1)} %multiply_reduce_fusion.3), channel_id=1, replica_groups=mesh['hyd'=4,'src'=8] {'src'}, use_global_device_ids=true, to_apply=%region_14.16 | all-reduce | flops 128 | bytes 1024 | tf_op jit(solution)/shard_map/psum | solution.py:101
  556.9 37.4 %while.63 = (s32[]{:T(128)}, f32[2,8,128,128]{3,2,1,0:T(8,128)}, s32[]{:T(128)}, s32[24]{0:T(128)S(1)}, bf16[24,2,128,128]{3,2,0,1:T(8,128)(2,1)S(1)}, /*index=5...) while((s32[]{:T(128)}, f32[2,8,128,128]{3,2,1,0:T(8,128)}, ...), condition=%wide.region_16.18_spmd, body=%wide.region_15.17_spmd.sunk | while | flops 135529568 | bytes 17834880 | solution.py:47
  563.7 2.2 fusion.398
  571.6 2.3 fusion.400
  575.9 2.2 fusion.401
  580.1 2.2 fusion.402
  584.0 2.2 fusion.403
  588.0 2.2 fusion.404
  592.1 2.2 fusion.405
  594.4 153.0 %all-gather.6.cloned.1.call-done = f32[8,2,1024,128]{3,2,1,0:T(8,128)} async-done(((f32[1,2,1024,128]{3,2,1,0:T(8,128)}), f32[8,2,1024,128]{3,2,1,0:T(8,128)}) %all-gather.6.cloned.1.call-update) | async-done | bytes 8388624 | tf_op jit(solution)/shard_map/all_gather | solution.py:113
  747.4 4.9 reduce_sum.85
  753.9 9.8 psum.68
  763.7 2.9 fusion.243
  767.6 41.2 %while.64 = (s32[]{:T(128)}, f32[2,8,128,128]{3,2,1,0:T(8,128)}, s32[]{:T(128)}, s32[24]{0:T(128)S(1)}, bf16[24,2,128,128]{2,3,0,1:T(8,128)(2,1)}, /*index=5*/s3...) while((s32[]{:T(128)}, f32[2,8,128,128]{3,2,1,0:T(8,128)}, ...), condition=%wide.region_21.23_spmd, body=%wide.region_20.22_spmd.sunk | while | flops 135529568 | bytes 17834880 | solution.py:81
  778.2 2.2 fusion.413
  786.1 2.3 fusion.415
  790.4 2.2 fusion.416
  794.6 2.2 fusion.417
  798.5 2.2 fusion.418
  802.5 2.2 fusion.419
  806.6 2.2 fusion.420
  808.9 129.7 %all-reduce.8.cloned.1.call-done = f32[2,1024,128]{2,1,0:T(8,128)} async-done(((f32[2,1024,128]{2,1,0:T(8,128)}), f32[2,1024,128]{2,1,0:T(8,128)}) %all-reduce.8.cloned.1.call-update) | async-done | bytes 1048592 | tf_op jit(solution)/shard_map/psum | solution.py:100
  940.1 16.2 %psum.70 = f32[128]{0:T(128)S(1)} all-reduce(f32[128]{0:T(128)S(1)} %multiply_reduce_fusion.1), channel_id=1, replica_groups=mesh['hyd'=4,'src'=8] {'src'}, use_global_device_ids=true, to_apply=%region_24.26 | all-reduce | flops 128 | bytes 1024 | tf_op jit(solution)/shard_map/psum | solution.py:101
  956.3 2.5 fusion.240
  959.9 37.5 %while.65 = (s32[]{:T(128)}, f32[2,8,128,128]{3,2,1,0:T(8,128)}, s32[]{:T(128)}, s32[24]{0:T(128)S(1)}, bf16[24,2,128,128]{3,2,0,1:T(8,128)(2,1)S(1)}, /*index=5...) while((s32[]{:T(128)}, f32[2,8,128,128]{3,2,1,0:T(8,128)}, ...), condition=%wide.region_26.28_spmd, body=%wide.region_25.27_spmd.sunk | while | flops 135529568 | bytes 17834880 | solution.py:47
  966.8 2.2 fusion.428
  970.7 2.2 fusion.429
  975.0 2.1 fusion.430
  978.8 2.2 fusion.431
  982.9 2.2 fusion.432
  986.9 2.2 fusion.433
  991.0 2.2 fusion.434
  995.1 2.3 fusion.435
  997.4 153.4 %all-gather.8.cloned.1.call-done = f32[8,2,1024,128]{3,2,1,0:T(8,128)} async-done(((f32[1,2,1024,128]{3,2,1,0:T(8,128)}), f32[8,2,1024,128]{3,2,1,0:T(8,128)}) %all-gather.8.cloned.1.call-update) | async-done | bytes 8388624 | tf_op jit(solution)/shard_map/all_gather | solution.py:113
  1150.8 4.9 reduce_sum.88
  1157.4 9.8 psum.71
  1167.2 3.6 multiply_subtract_fusion
  (128 shorter events, 68.5 us)
Async XLA Ops:
  7.2 142.2 %all-reduce.4.cloned.1.call-start = ((), (), s32[]{:S(2)}) async-start(), calls=%async_computation | async-start | bytes 2097152 | tf_op jit(solution)/shard_map/psum | solution.py:100
  7.9 2.8 copy-start.7
  10.6 0.7 copy-start.8
  10.6 0.7 copy-start.9
  39.0 1.0 copy-start
  40.0 307.3 %all-gather.4.cloned.1.call-start = ((), (), s32[]{:S(2)}) async-start(), calls=%async_computation.1 | async-start | bytes 9437184 | tf_op jit(solution)/shard_map/all_gather | solution.py:113
  190.7 345.4 %all-reduce.6.cloned.1.call-start = ((), (), s32[]{:S(2)}) async-start(), calls=%async_computation.2 | async-start | bytes 2097152 | tf_op jit(solution)/shard_map/psum | solution.py:100
  351.2 12.2 %copy-start.1 = (f32[2,1024,128]{2,1,0:T(8,128)}, f32[2,1024,128]{2,1,0:T(8,128)S(1)}, u32[]{:S(2)}) copy-start(f32[2,1024,128]{2,1,0:T(8,128)S(1)} %reduce_sum.82) | copy-start | bytes 3145732
  405.9 147.9 %copy-start.3 = (f32[2,1024,128]{2,1,0:T(8,128)S(1)}, f32[2,1024,128]{2,1,0:T(8,128)}, u32[]{:S(2)}) copy-start(f32[2,1024,128]{2,1,0:T(8,128)} %all-reduce.4.cloned.1.call-done) | copy-start | bytes 3145732
  405.9 341.5 %all-gather.6.cloned.1.call-start = ((), (), s32[]{:S(2)}) async-start(), calls=%async_computation.3 | async-start | bytes 9437184 | tf_op jit(solution)/shard_map/all_gather | solution.py:113
  594.3 344.3 %all-reduce.8.cloned.1.call-start = ((), (), s32[]{:S(2)}) async-start(), calls=%async_computation.4 | async-start | bytes 2097152 | tf_op jit(solution)/shard_map/psum | solution.py:100
  752.3 11.4 copy-start.2
  808.8 147.5 %copy-start.4 = (f32[2,1024,128]{2,1,0:T(8,128)S(1)}, f32[2,1024,128]{2,1,0:T(8,128)}, u32[]{:S(2)}) copy-start(f32[2,1024,128]{2,1,0:T(8,128)} %all-reduce.4.cloned.1.call-done) | copy-start | bytes 3145732
  808.8 342.0 %all-gather.8.cloned.1.call-start = ((), (), s32[]{:S(2)}) async-start(), calls=%async_computation.5 | async-start | bytes 9437184 | tf_op jit(solution)/shard_map/all_gather | solution.py:113
  1150.8 16.4 %copy-start.6 = (f32[2,1024,128]{2,1,0:T(8,128)S(1)}, f32[2,1024,128]{2,1,0:T(8,128)}, u32[]{:S(2)}) copy-start(f32[2,1024,128]{2,1,0:T(8,128)} %all-reduce.6.cloned.1.call-done) | copy-start | bytes 3145732
  1155.8 11.5 copy-start.5
Sparse Core Ops, SparseCore 0:
  40.1 109.1 all-reduce.3
  190.8 156.4 all-gather.3
  406.0 129.9 all-reduce.5
  594.4 152.9 all-gather.5
  809.0 129.5 all-reduce.7
  997.5 153.2 all-gather.7
